TPU v7x, 32 devices: a whole 2x2x4 slice. The times are simulated.
32 devices in a mesh: section: 2 (over core), dp: 16 (over z, y, x).
Axes of the slice: x: 2, y: 2, z: 4, core: 2. Of those that a mesh axis runs over, the one named last changes fastest.
Arguments:
- byte_states: bfloat16 [32768, 768], P('dp'), may hold values from -6 to 6
- lengths: int32 [32], P('dp'), may hold values from 512 to 1024, as said below
- patch_weight: bfloat16 [6144, 768], replicated, may hold values from -0.078125 to 0.078125
- qkv_weight: bfloat16 [2, 768, 2304], P('section'), may hold values from -0.21875 to 0.21875
- out_weight: bfloat16 [2, 768, 768], P('section'), may hold values from -0.875 to 0.875
- up_weight: bfloat16 [2, 768, 3072], P('section'), may hold values from -0.21875 to 0.21875
- down_weight: bfloat16 [2, 3072, 768], P('section'), may hold values from -0.109375 to 0.109375
- norm_gains: float32 [2, 2, 768], P('section'), may hold values from 0.25 to 1.75
- byte_cotangent: bfloat16 [32768, 768], P('dp'), may hold values from -6 to 6
Outputs:
- section_outputs: bfloat16 [2, 32768, 768], P('section', 'dp')
- input_grad: float32 [32768, 768], P('dp')
- patch_grad: float32 [6144, 768], P(('section', 'dp'))
- qkv_grad: float32 [2, 768, 2304], P('section', 'dp')
- proj_grad: float32 [2, 768, 768], P('section', 'dp')
- up_grad: float32 [2, 768, 3072], P('section', 'dp')
- down_grad: float32 [2, 3072, 768], P('section', 'dp')
- gain_grad: float32 [2, 2, 768], P('section', None, 'dp')
Inputs may be any that keep to these rules, and one draw needn't show every extreme that they name: `lengths`: each a multiple of 8; some sequence has all 1024 bytes live in every draw.
All inputs are finite; a program needn't handle non-finite values.
Results may differ from a plain program's by a relative error of at most 0.02.
Values may be sent and summed in bfloat16 or wider, within the bound.
A program may use at most 384 MiB of HBM per device.

v0:
```python
import functools

import jax
import jax.numpy as jnp
from jax import lax
from jax.experimental import pallas as pl
from jax.experimental.pallas import tpu as pltpu
from jax.sharding import PartitionSpec as P

D = 768
HEADS = 12
HDIM = 64
FF = 3072
PATCH = 8
SEQ = 1024
PATCHES = SEQ // PATCH
TILE = 256
SUBS = TILE // 128
PAIRS = HEADS // 2
TILES = SEQ // TILE
MB = 2
XG = 3 * D + FF
F32 = jnp.float32
BF16 = jnp.bfloat16
ANY = pl.BlockSpec(memory_space=pl.ANY)
VLIMIT = 56 * 2**20


def sds(shape, dtype):
    return jax.ShapeDtypeStruct(shape, dtype)


def mm(a, b):
    return jnp.dot(a, b, preferred_element_type=F32)


def mm_nt(a, b):
    return lax.dot_general(a, b, (((1,), (1,)), ((), ())), preferred_element_type=F32)


def mm_tn(a, b):
    return lax.dot_general(a, b, (((0,), (0,)), ((), ())), preferred_element_type=F32)


def lanes(start, size):
    return pl.ds(pl.multiple_of(start, 128), size)


def normalized(v):
    centered = v - jnp.mean(v, axis=-1, keepdims=True)
    scale = lax.rsqrt(jnp.mean(centered * centered, axis=-1, keepdims=True) + 1e-5)
    return centered * scale, scale


def norm_backward(grad, gain, hat, scale):
    scaled = grad * gain
    inner = scaled - jnp.mean(scaled, axis=-1, keepdims=True)
    inner = inner - hat * jnp.mean(scaled * hat, axis=-1, keepdims=True)
    return inner * scale, jnp.sum(grad * hat, axis=0, keepdims=True)


def gelu_pair(z):
    cdf = 0.5 + 0.5 * lax.erf(z * 0.7071067811865476)
    bell = jnp.exp2(z * z * (-0.5 * 1.4426950408889634))
    return z * cdf, cdf + z * (bell * 0.3989422804014327)


def lane_masks():
    lane = lax.broadcasted_iota(jnp.int32, (128, 128), 1)
    first = jnp.where(lane < HDIM, 1.0, 0.0)
    return first.astype(BF16), (1.0 - first).astype(BF16), lane < HDIM


def split_heads(v, first, second):
    return jnp.concatenate([v * first, v * second], axis=0)


def attention_forward(qkv_ref, o_ref, p_ref, shift):
    first, second, _ = lane_masks()
    key = lax.broadcasted_iota(jnp.int32, (128, 128), 0)
    query = lax.broadcasted_iota(jnp.int32, (128, 128), 1)
    allowed = (key <= query) & ((key >> shift) == (query >> shift))

    @pl.loop(0, SUBS)
    def _(sub):
        rows = pl.ds(pl.multiple_of(sub * 128, 128), 128)
        scores, probs = [], []
        for lo in range(0, D, 128):
            k2 = split_heads(qkv_ref[rows, D + lo : D + lo + 128], first, second)
            scores.append(mm_nt(k2, qkv_ref[rows, lo : lo + 128]) * 0.125)
        for pair in range(PAIRS):
            parts = []
            for half in range(2):
                sh = jnp.where(allowed, scores[pair][half * 128 : half * 128 + 128], -1e30)
                e = jnp.exp(sh - jnp.max(sh, axis=0, keepdims=True))
                parts.append(e * (1.0 / jnp.sum(e, axis=0, keepdims=True)))
            probs.append(jnp.concatenate(parts, axis=0).astype(BF16))
            p_ref[sub, pair] = probs[pair]
        for pair in range(PAIRS):
            lo = pair * 128
            v2 = split_heads(qkv_ref[rows, 2 * D + lo : 2 * D + lo + 128], first, second)
            o_ref[rows, lo : lo + 128] = mm_tn(probs[pair], v2).astype(BF16)


def attention_backward(qkv_ref, p_ref, do_ref, dqkv_ref):
    first, second, is_first = lane_masks()

    @pl.loop(0, SUBS)
    def _(sub):
        rows = pl.ds(pl.multiple_of(sub * 128, 128), 128)
        dps, dss = [], []
        for lo in range(0, D, 128):
            v2 = split_heads(qkv_ref[rows, 2 * D + lo : 2 * D + lo + 128], first, second)
            dps.append(mm_nt(v2, do_ref[rows, lo : lo + 128]))
        for pair in range(PAIRS):
            pf = p_ref[sub, pair].astype(F32)
            weighted = pf * dps[pair]
            parts = []
            for half in range(2):
                keys = slice(half * 128, half * 128 + 128)
                parts.append(weighted[keys] - pf[keys] * jnp.sum(weighted[keys], axis=0, keepdims=True))
            dss.append(jnp.concatenate(parts, axis=0).astype(BF16))
        for pair in range(PAIRS):
            lo = pair * 128
            k2 = split_heads(qkv_ref[rows, D + lo : D + lo + 128], first, second)
            dq = mm_tn(dss[pair], k2) * 0.125
            dk2 = mm(dss[pair], qkv_ref[rows, lo : lo + 128]) * 0.125
            dv2 = mm(p_ref[sub, pair], do_ref[rows, lo : lo + 128])
            dqkv_ref[rows, lo : lo + 128] = dq.astype(BF16)
            dqkv_ref[rows, D + lo : D + lo + 128] = jnp.where(is_first, dk2[:128], dk2[128:]).astype(BF16)
            dqkv_ref[rows, 2 * D + lo : 2 * D + lo + 128] = jnp.where(is_first, dv2[:128], dv2[128:]).astype(BF16)


def block_forward(
    h, gains, w, wait, shift, a_ref, qkv_ref, p_ref, o_ref, mid_ref, c_ref, u_ref, gp_ref, done=lambda i: None
):
    wq, wo, wu, wd = w
    a_ref[...] = (normalized(h)[0] * gains[0:1, :]).astype(BF16)
    wait(0)

    @pl.loop(0, 3)
    def _(part):
        cols = lanes(part * D, D)
        qkv_ref[:, cols] = mm(a_ref[...], wq[:, cols]).astype(BF16)

    attention_forward(qkv_ref, o_ref, p_ref, shift)
    done(0)
    wait(1)
    mid = h + mm(o_ref[...], wo[...])
    mid_ref[...] = mid
    c_ref[...] = (normalized(mid)[0] * gains[1:2, :]).astype(BF16)
    done(1)
    wait(2)

    @pl.loop(0, FF // D)
    def _(part):
        cols = lanes(part * D, D)
        u, gp = gelu_pair(mm(c_ref[...], wu[:, cols]))
        u_ref[:, cols] = u.astype(BF16)
        gp_ref[:, cols] = gp.astype(BF16)

    done(2)
    wait(3)
    return mid_ref[...] + mm(u_ref[...], wd[...])


def dz_product(dm, wd, gp_ref, dz_ref):
    @pl.loop(0, FF // D)
    def _(part):
        cols = lanes(part * D, D)
        du = mm_nt(dm, wd[pl.ds(pl.multiple_of(part * D, D), D), :])
        dz_ref[:, cols] = (du * gp_ref[:, cols].astype(F32)).astype(BF16)


def backward_upper(dout, gains, wo, wu, dz_ref, mid_ref, dr_ref, do_ref, dmid_ref):
    hat, scale = normalized(mid_ref[...])
    dc = mm_nt(dz_ref[...], wu[...])
    back, dgain = norm_backward(dc, gains[1:2, :], hat, scale)
    dmid_ref[...] = dout + back
    dr_ref[...] = dmid_ref[...].astype(BF16)
    do_ref[...] = mm_nt(dr_ref[...], wo[...]).astype(BF16)
    return dgain


def backward_lower(h, gains, wq, qkv_ref, p_ref, do_ref, dqkv_ref, dmid_ref):
    attention_backward(qkv_ref, p_ref, do_ref, dqkv_ref)
    da = mm_nt(dqkv_ref[...], wq[...])
    hat, scale = normalized(h)
    back, dgain = norm_backward(da, gains[0:1, :], hat, scale)
    return dmid_ref[...] + back, dgain


def block_backward(dout, h, gains, w, wait, dz_ref, mid_ref, qkv_ref, p_ref, do_ref, dr_ref, dqkv_ref, dmid_ref):
    wq, wo, wu = w
    for i in (2, 1, 0):
        wait(i)
    dgain_two = backward_upper(dout, gains, wo, wu, dz_ref, mid_ref, dr_ref, do_ref, dmid_ref)
    dh, dgain_one = backward_lower(h, gains, wq, qkv_ref, p_ref, do_ref, dqkv_ref, dmid_ref)
    return dh, jnp.concatenate([dgain_one, dgain_two], axis=0)


LANES = D // 128


def fill_lanes(dst, src):
    for b in range(LANES):
        dst[b] = src[:, b * 128 : b * 128 + 128].astype(F32)


def strided_rows(ref, start, rows):
    picked = [ref[b, pl.ds(start, rows, stride=PATCH), :] for b in range(LANES)]
    return jnp.concatenate(picked, axis=1)


def spread_matrix():
    row = lax.broadcasted_iota(jnp.int32, (TILE, TILE // PATCH), 0) // PATCH
    col = lax.broadcasted_iota(jnp.int32, (TILE, TILE // PATCH), 1)
    return jnp.where(row == col, 1.0, 0.0).astype(BF16)


def add_low(a, b):
    return (a.astype(F32) + b.astype(F32)).astype(BF16)


def cost(flops, nbytes):
    return pl.CostEstimate(flops=int(flops), bytes_accessed=int(nbytes), transcendentals=0)


WSCRATCH = {
    "q": pltpu.VMEM((D, 3 * D), BF16),
    "o": pltpu.VMEM((D, D), BF16),
    "u": pltpu.VMEM((D, FF), BF16),
    "d": pltpu.VMEM((FF, D), BF16),
}


CORE, X, Y, ZN, ZF, XY = range(6)
QKV, OUT, UP, DOWN = range(4)
ROWS_OF = (D // 16, D // 16, D // 16, FF // 16)
HALF_OF = (3 * D // 2, D // 2, FF // 2, D // 2)
X_LO = (0, D, 2 * D, 3 * D)
DY_LO = (0, 3 * D // 2, 2 * D, 2 * D + FF // 2)
WIDTH_G = (3 * D + D + FF + D) // 2
ROWS_G = MB * PATCHES
UNIT = 384
MESH_ID = pl.DeviceIdType.MESH


class Net:
    def __init__(self, send, recv, local):
        self.send, self.recv, self.local, self.count, self.local_count = send, recv, local, 0, 0
        self.core = lax.axis_index("section")
        at = lax.axis_index("dp")
        self.x, self.y, self.z = at % 2, (at // 2) % 2, at // 4
        self.z0, self.z1 = self.z % 2, self.z // 2
        z0, z1 = self.z0, self.z1
        spot = lambda x, y, z: {"dp": z * 4 + y * 2 + x}
        self.partner = (
            {"section": 1 - self.core}, spot(1 - self.x, self.y, self.z), spot(self.x, 1 - self.y, self.z),
            spot(self.x, self.y, 1 - z0 + 2 * z1), spot(self.x, self.y, z0 + 2 - 2 * z1),
            spot(1 - self.x, 1 - self.y, self.z),
        )

    def meet(self):
        barrier = pltpu.get_barrier_semaphore()
        for device in self.partner:
            pl.semaphore_signal(barrier, inc=1, device_id=device, device_id_type=MESH_ID)
        pl.semaphore_wait(barrier, len(self.partner))

    def remote(self, src, dst, to):
        n = self.count
        self.count += 1
        return pltpu.make_async_remote_copy(
            src_ref=src, dst_ref=dst, send_sem=self.send.at[n], recv_sem=self.recv.at[n],
            device_id=self.partner[to], device_id_type=MESH_ID,
        )

    def load(self, src, dst):
        n = self.local_count
        self.local_count += 1
        return pltpu.make_async_copy(src, dst, self.local.at[n])

    def on(self, which, fn):
        pl.when(self.core == which)(fn)

    def z_of(self, k):
        return (self.z0 + k % 2) % 2 + 2 * ((self.z1 + k // 2) % 2)


def global_forward_kernel(
    bytes_ref, gains_ref, wp_hbm, wq_hbm, wo_hbm, wu_hbm, wd_hbm,
    own_out, g_out, x_out, start_out, qkv_out, p_out, mid_out, gp_out, pat_out,
    bytes_f32, wp, wq, wo, wu, wd, x_s, start_s, qkv_s, p_s, mid_s, gp_s, pat_s, g_s, psem, wsem, osem, send, recv,
):
    net = Net(send, recv, osem)
    core = net.core
    barrier = pltpu.get_barrier_semaphore()
    pl.semaphore_signal(barrier, inc=1, device_id=net.partner[CORE], device_id_type=MESH_ID)

    def wp_copy(j):
        rows = pl.ds(pl.multiple_of(j * D, D), D)
        return pltpu.make_async_copy(wp_hbm.at[rows, :], wp.at[rows, :], psem.at[j])

    wcopies = [
        pltpu.make_async_copy(src.at[0], dst, wsem.at[i])
        for i, (src, dst) in enumerate(((wq_hbm, wq), (wo_hbm, wo), (wu_hbm, wu), (wd_hbm, wd)))
    ]

    def start_weights():
        for j in range(PATCH):
            wp_copy(j).start()
        for copy in wcopies:
            copy.start()

    net.on(0, start_weights)
    fill_lanes(bytes_f32, bytes_ref)
    start_s[...] = jnp.zeros_like(start_s)

    @pl.loop(0, PATCH)
    def _(j):
        mine = j // (PATCH // 2) == core

        @pl.when((core == 0) | mine)
        def _():
            xj = strided_rows(bytes_f32, j, ROWS_G).astype(BF16)

            @pl.when(core == 0)
            def _():
                wp_copy(j).wait()
                start_s[...] = start_s[...] + mm(xj, wp[pl.ds(pl.multiple_of(j * D, D), D), :])

            @pl.when(mine)
            def _():
                for piece in range(4):
                    xr = 1 - net.x if piece % 2 else net.x
                    yr = 1 - net.y if piece // 2 else net.y
                    pat_s[yr * 2 + xr, j % (PATCH // 2)] = xj[:, piece * 192 : piece * 192 + 192]

    pat_copy = net.load(pat_s, pat_out)
    pat_copy.start()
    pl.semaphore_wait(barrier, 1)
    outs = [
        net.load(*pair) for pair in (
            (start_s, start_out), (qkv_s, qkv_out), (p_s, p_out), (mid_s, mid_out), (gp_s, gp_out), (x_s, x_out),
            (g_s, g_out), (g_s.at[0:PATCHES, :], own_out),
        )
    ]
    give = net.remote(g_s.at[PATCHES:ROWS_G, :], own_out, CORE)

    def work():
        moved = pltpu.roll(start_s[...], 1, 0)
        row = lax.broadcasted_iota(jnp.int32, (ROWS_G, D), 0)
        start_s[...] = jnp.where((row & (PATCHES - 1)) == 0, 0.0, moved)
        outs[0].start()

        def done(i):
            for copy in ((outs[1], outs[2]), (outs[3],), (outs[4], outs[5]))[i]:
                copy.start()

        out = block_forward(
            start_s[...], gains_ref[0], (wq, wo, wu, wd), lambda i: wcopies[i].wait(), 7,
            x_s.at[:, 0:D], qkv_s, p_s, x_s.at[:, D : 2 * D], mid_s,
            x_s.at[:, 2 * D : 3 * D], x_s.at[:, 3 * D : 3 * D + FF], gp_s, done,
        )
        g_s[...] = out.astype(BF16)
        give.start()
        outs[6].start()
        outs[7].start()
        for copy in outs:
            copy.wait()
        give.wait_send()

    net.on(0, work)
    net.on(1, give.wait_recv)
    pat_copy.wait()


def global_forward(states, gains, patch_weight, weights):
    outs = (
        ((PATCHES, D), BF16), ((ROWS_G, D), BF16), ((ROWS_G, XG), BF16), ((ROWS_G, D), F32), ((ROWS_G, 3 * D), BF16),
        ((SUBS, PAIRS, 256, 128), BF16), ((ROWS_G, D), F32), ((ROWS_G, FF), BF16), ((4, PATCH // 2, ROWS_G, 192), BF16),
    )
    vmem = pl.BlockSpec(memory_space=pltpu.VMEM)
    held = [pltpu.VMEM(*o) for o in outs[2:]] + [pltpu.VMEM((ROWS_G, D), BF16)]
    return pl.pallas_call(
        global_forward_kernel,
        name="global_forward",
        out_shape=[sds(*o) for o in outs],
        in_specs=[vmem] * 2 + [ANY] * 5,
        out_specs=[ANY] * len(outs),
        scratch_shapes=[
            pltpu.VMEM((LANES, MB * SEQ, 128), F32), pltpu.VMEM((PATCH * D, D), BF16),
            WSCRATCH["q"], WSCRATCH["o"], WSCRATCH["u"], WSCRATCH["d"], *held,
            pltpu.SemaphoreType.DMA((PATCH,)), pltpu.SemaphoreType.DMA((4,)), pltpu.SemaphoreType.DMA((9,)),
            pltpu.SemaphoreType.DMA((1,)), pltpu.SemaphoreType.DMA((1,)),
        ],
        compiler_params=pltpu.CompilerParams(vmem_limit_bytes=VLIMIT, collective_id=3, has_side_effects=True),
        cost_estimate=cost(6e9, 32e6),
    )(states, gains, patch_weight, *weights)


def global_backward_kernel(
    scal, dg0_ref, dg1_ref, start_ref, mid_ref, qkv_ref, p_ref, gp_ref, gains_ref, wq_hbm, wo_hbm, wu_hbm, wd_hbm,
    dpp_ref, keep_ref, send_ref, dgain_ref,
    dm_s, dz_s, do_s, dr_s, dqkv_s, dmid_s, wq, wo, wu, wd, wsem,
):
    @pl.when(scal[0] == 0)
    def _():
        rows = MB * PATCHES
        wcopies = [
            pltpu.make_async_copy(src.at[0], dst, wsem.at[i])
            for i, (src, dst) in enumerate(((wq_hbm, wq), (wo_hbm, wo), (wu_hbm, wu), (wd_hbm, wd)))
        ]
        for i in (3, 2, 1, 0):
            wcopies[i].start()
        dm_s[0:PATCHES, :] = dg0_ref[...]
        dm_s[PATCHES:, :] = dg1_ref[...]
        wcopies[3].wait()
        dz_product(dm_s[...], wd, gp_ref, dz_s)
        dh, dgain = block_backward(
            dm_s[...].astype(F32), start_ref[...], gains_ref[0], (wq, wo, wu), lambda i: wcopies[i].wait(),
            dz_s, mid_ref, qkv_ref, p_ref, do_s, dr_s, dqkv_s, dmid_s,
        )
        dgain_ref[...] = jnp.zeros_like(dgain_ref)
        dgain_ref[0:2, :] = dgain
        moved = pltpu.roll(dh, rows - 1, 0)
        row = lax.broadcasted_iota(jnp.int32, (rows, D), 0)
        dpp_ref[...] = jnp.where((row & (PATCHES - 1)) == PATCHES - 1, 0.0, moved).astype(BF16)
        for half in range(2):
            def fill(ref):
                lo = 0
                for src, width in ((dqkv_s, 3 * D // 2), (dr_s, D // 2), (dz_s, FF // 2), (dm_s, D // 2)):
                    ref[:, lo : lo + width] = src[:, half * width : half * width + width]
                    lo += width
            pl.when(scal[1] == half)(functools.partial(fill, keep_ref))
            pl.when(scal[1] != half)(functools.partial(fill, send_ref))

    @pl.when(scal[0] != 0)
    def _():
        dgain_ref[...] = jnp.zeros_like(dgain_ref)


def global_backward(scal, dgs, saved, gains, weights):
    rows = MB * PATCHES
    full = lambda *shape: pl.BlockSpec(shape, lambda i, s: (0,) * len(shape), pipeline_mode=pl.Buffered(1))
    width = (3 * D + D + FF + D) // 2
    outs = (((rows, D), BF16), ((rows, width), BF16), ((rows, width), BF16), ((8, D), F32))
    return pl.pallas_call(
        global_backward_kernel,
        name="global_backward",
        out_shape=[sds(*o) for o in outs],
        grid_spec=pltpu.PrefetchScalarGridSpec(
            num_scalar_prefetch=1,
            grid=(1,),
            in_specs=[full(PATCHES, D)] * 2 + [full(*v.shape) for v in saved] + [full(1, 2, D)] + [ANY] * 4,
            out_specs=[full(*o[0]) for o in outs],
            scratch_shapes=[
                pltpu.VMEM((rows, D), BF16), pltpu.VMEM((rows, FF), BF16), pltpu.VMEM((rows, D), BF16),
                pltpu.VMEM((rows, D), BF16), pltpu.VMEM((rows, 3 * D), BF16), pltpu.VMEM((rows, D), F32),
                WSCRATCH["q"], WSCRATCH["o"], WSCRATCH["u"], WSCRATCH["d"],
                pltpu.SemaphoreType.DMA((4,)),
            ],
        ),
        compiler_params=pltpu.CompilerParams(vmem_limit_bytes=VLIMIT),
        cost_estimate=cost(6e9, 24e6),
    )(scal, *dgs, *saved, gains, *weights)


def start_weights(scal, pairs, sems, order):
    step = pl.program_id(0)
    for i in order:
        own, recv, dst = pairs[i]

        @pl.when((step == 0) & (scal[0] == 1))
        def _(own=own, dst=dst, i=i):
            pltpu.make_async_copy(own.at[0], dst, sems.at[i]).start()

        @pl.when((step == 0) & (scal[0] == 0))
        def _(recv=recv, dst=dst, i=i):
            pltpu.make_async_copy(recv.at[0], dst, sems.at[i]).start()

    def wait(i):
        @pl.when(step == 0)
        def _():
            pltpu.make_async_copy(pairs[i][1].at[0], pairs[i][2], sems.at[i]).wait()

    return wait


def live_rows(scal):
    step = pl.program_id(0)
    row = lax.broadcasted_iota(jnp.int32, (TILE, D), 0) + step * TILE
    return row < scal[4]


def local_forward_kernel(
    scal, bytes_ref, cot_ref, g_ref, gains_ref, wq_a, wo_a, wu_a, wd_a, wq_b, wo_b, wu_b, wd_b, gains_b,
    y_ref, dm_ref, a_ref, qkv_ref, p_ref, o_ref, mid_ref, c_ref, u_ref, gp_ref,
    wq, wo, wu, wd, wsem,
):
    pairs = ((wq_a, wq_b, wq), (wo_a, wo_b, wo), (wu_a, wu_b, wu), (wd_a, wd_b, wd))
    wait = start_weights(scal, pairs, wsem, (0, 1, 2, 3))
    gains = jnp.where(scal[0] == 1, gains_ref[0], gains_b[0])
    h = bytes_ref[...].astype(F32) + mm(spread_matrix(), g_ref[...])
    out = block_forward(h, gains, (wq, wo, wu, wd), wait, 3, a_ref, qkv_ref, p_ref, o_ref, mid_ref, c_ref, u_ref, gp_ref)
    live = live_rows(scal)
    y_ref[...] = jnp.where(live, out, 0.0).astype(BF16)
    dm_ref[...] = jnp.where(live, cot_ref[...].astype(F32), 0.0).astype(BF16)


def row_block(*shape):
    return pl.BlockSpec(shape, lambda i, s: (i,) + (0,) * (len(shape) - 1))


def const_block(*shape):
    return pl.BlockSpec(shape, lambda i, s: (0,) * len(shape), pipeline_mode=pl.Buffered(1))


def seq_block():
    return pl.BlockSpec((TILE, D), lambda i, s: (s[0] * TILES + i, 0))


def local_forward(scal, states, cotangent, g_own, gains, weights, gains_b, weights_b):
    outs = (
        ((SEQ, D), BF16), ((SEQ, D), BF16), ((SEQ, D), BF16), ((SEQ, 3 * D), BF16),
        ((SEQ // 128, PAIRS, 256, 128), BF16), ((SEQ, D), BF16), ((SEQ, D), F32), ((SEQ, D), BF16),
        ((SEQ, FF), BF16), ((SEQ, FF), BF16),
    )
    return pl.pallas_call(
        local_forward_kernel,
        name="local_forward",
        out_shape=[sds(*o) for o in outs],
        grid_spec=pltpu.PrefetchScalarGridSpec(
            num_scalar_prefetch=1,
            grid=(TILES,),
            in_specs=[seq_block(), seq_block(), row_block(TILE // PATCH, D), const_block(1, 2, D)]
            + [ANY] * 8 + [const_block(1, 2, D)],
            out_specs=[row_block(o[0][0] // TILES, *o[0][1:]) for o in outs],
            scratch_shapes=[
                WSCRATCH["q"], WSCRATCH["o"], WSCRATCH["u"], WSCRATCH["d"], pltpu.SemaphoreType.DMA((4,)),
            ],
        ),
        compiler_params=pltpu.CompilerParams(vmem_limit_bytes=VLIMIT),
        cost_estimate=cost(14.5e9, 60e6),
    )(scal, states, cotangent, g_own, gains, *weights, *weights_b, gains_b)


def local_dz_kernel(scal, dm_ref, gp_ref, wd_a, wd_b, dz_ref, wd, wsem):
    wait = start_weights(scal, ((wd_a, wd_b, wd),), wsem, (0,))
    wait(0)
    dz_product(dm_ref[...], wd, gp_ref, dz_ref)


def local_dz(scal, dm, gp, wd_a, wd_b):
    return pl.pallas_call(
        local_dz_kernel,
        name="local_dz",
        out_shape=sds((SEQ, FF), BF16),
        grid_spec=pltpu.PrefetchScalarGridSpec(
            num_scalar_prefetch=1,
            grid=(TILES,),
            in_specs=[row_block(TILE, D), row_block(TILE, FF), ANY, ANY],
            out_specs=row_block(TILE, FF),
            scratch_shapes=[WSCRATCH["d"], pltpu.SemaphoreType.DMA((1,))],
        ),
        compiler_params=pltpu.CompilerParams(vmem_limit_bytes=VLIMIT),
        cost_estimate=cost(4.8e9, 18e6),
    )(scal, dm, gp, wd_a, wd_b)


def local_backward_kernel(
    scal, dz_ref, dm_ref, bytes_ref, g_ref, mid_ref, qkv_ref, p_ref, gains_ref,
    wq_a, wo_a, wu_a, wq_b, wo_b, wu_b, gains_b,
    dr_ref, dqkv_ref, dh_ref, dg_ref, dgain_ref,
    do_s, wq, wo, wu, wsem,
):
    pairs = ((wq_a, wq_b, wq), (wo_a, wo_b, wo), (wu_a, wu_b, wu))
    wait = start_weights(scal, pairs, wsem, (2, 1, 0))
    gains = jnp.where(scal[0] == 1, gains_ref[0], gains_b[0])
    h = bytes_ref[...].astype(F32) + mm(spread_matrix(), g_ref[...])
    dh, dgain = block_backward(
        dm_ref[...].astype(F32), h, gains, (wq, wo, wu), wait, dz_ref, mid_ref, qkv_ref, p_ref, do_s, dr_ref, dqkv_ref,
        dh_ref,
    )
    dh_ref[...] = dh
    dg_ref[...] = jnp.sum(dh.reshape(TILE // PATCH, PATCH, D), axis=1).astype(BF16)

    @pl.when(pl.program_id(0) == 0)
    def _():
        dgain_ref[...] = jnp.zeros_like(dgain_ref)

    dgain_ref[0:2, :] += dgain


def local_backward(scal, dz, dm, states, g_own, mid, qkv, p, gains, weights, gains_b, weights_b):
    outs = (
        ((SEQ, D), BF16), ((SEQ, 3 * D), BF16), ((SEQ, D), F32), ((PATCHES, D), BF16), ((8, D), F32),
    )
    return pl.pallas_call(
        local_backward_kernel,
        name="local_backward",
        out_shape=[sds(*o) for o in outs],
        grid_spec=pltpu.PrefetchScalarGridSpec(
            num_scalar_prefetch=1,
            grid=(TILES,),
            in_specs=[
                row_block(TILE, FF), row_block(TILE, D), seq_block(), row_block(TILE // PATCH, D), row_block(TILE, D),
                row_block(TILE, 3 * D), row_block(SUBS, PAIRS, 256, 128), const_block(1, 2, D),
            ] + [ANY] * 6 + [const_block(1, 2, D)],
            out_specs=[row_block(o[0][0] // TILES, *o[0][1:]) for o in outs[:4]] + [const_block(8, D)],
            scratch_shapes=[
                pltpu.VMEM((TILE, D), BF16), WSCRATCH["q"], WSCRATCH["o"], WSCRATCH["u"], pltpu.SemaphoreType.DMA((3,)),
            ],
        ),
        compiler_params=pltpu.CompilerParams(vmem_limit_bytes=VLIMIT),
        cost_estimate=cost(10e9, 50e6),
    )(scal, dz, dm, states, g_own, mid, qkv, p, gains, *weights, *weights_b, gains_b)


def store_shards(scal, total, keep_ref, send_ref, add_refs, order, r, count, z):
    first, second = order
    position = {"x": scal[1], "y": scal[2]}
    for one in range(2):
        for two in range(2):
            at = {first: one ^ position[first], second: two ^ position[second]}
            for k in range(count // 4):
                level = (k ^ scal[3]) * 4 if count == 16 else 0
                shard = level + at["y"] * 2 + at["x"]
                value = total[pl.ds(pl.multiple_of(shard * r, 16), r), :]
                if add_refs is not None:
                    value = value + add_refs[one][two, k].astype(F32)
                (send_ref if one else keep_ref)[two, k] = value.astype(BF16)


def weight_grad_kernel(scal, *refs, parts, order, r, count, has_add, core_zero, shards):
    xs, dys, refs = refs[:parts], refs[parts : 2 * parts], refs[2 * parts :]
    adds = None
    if has_add:
        adds, refs = refs[:2], refs[2:]

    def work():
        value = mm_tn(xs[0][...], dys[0][...])
        for x, dy in zip(xs[1:], dys[1:]):
            value = value + mm_tn(x[...], dy[...])
        if not shards:
            refs[0][...] = value
            return
        keep_ref, send_ref, total = refs
        total[...] = value
        store_shards(scal, total, keep_ref, send_ref, adds, order, r, count, pl.program_id(0))

    if core_zero:
        pl.when(scal[0] == 0)(work)
    else:
        work()


def weight_grad(scal, xs, x_lo, dys, dy_lo, rows, cols, tn, order, add=None, half=None, core_zero=False, shards=True):
    mt, nt = rows // D, cols // tn
    r = rows // 16
    count = 16 if mt == 1 else 4
    depth = xs[0].shape[0]
    kz = 4 if mt == 1 else 1

    def dy_map(m, n, s):
        offset = 0 if half is None else (s[0] if half == "own" else 1 - s[0]) * nt
        return (0, dy_lo // tn + offset + n)

    shard_spec = pl.BlockSpec((2, kz, r, tn), lambda m, n, s: (0, 0 if mt == 1 else m ^ s[3], 0, n))
    if shards:
        out_shape = [sds((2, 4, r, cols), BF16)] * 2
        out_specs = [shard_spec] * 2
        scratch = [pltpu.VMEM((D, tn), F32)]
    else:
        out_shape = sds((rows, cols), F32)
        out_specs = pl.BlockSpec((D, tn), lambda m, n, s: (m, n))
        scratch = []
    return pl.pallas_call(
        functools.partial(
            weight_grad_kernel, parts=len(xs), order=order, r=r, count=count, has_add=add is not None,
            core_zero=core_zero, shards=shards,
        ),
        name="weight_grad",
        out_shape=out_shape,
        grid_spec=pltpu.PrefetchScalarGridSpec(
            num_scalar_prefetch=1,
            grid=(mt, nt),
            in_specs=[pl.BlockSpec((depth, D), lambda m, n, s: (0, x_lo // D + m))] * len(xs)
            + [pl.BlockSpec((depth, tn), dy_map)] * len(xs) + [shard_spec] * (0 if add is None else 2),
            out_specs=out_specs,
            scratch_shapes=scratch,
        ),
        compiler_params=pltpu.CompilerParams(vmem_limit_bytes=VLIMIT),
        cost_estimate=cost(2 * depth * len(xs) * rows * cols, 2 * (depth * (rows + cols) + rows * cols)),
    )(scal, *xs, *dys, *(add or ()))


def patch_grad_kernel(scal, bytes_ref, dpp_ref, *refs, order, shards):
    bytes_f32, total = refs[-2:]

    @pl.when(pl.program_id(0) == 0)
    def _():
        fill_lanes(bytes_f32, bytes_ref)

    byte = scal[0] * (PATCH // 2) + pl.program_id(0)
    x = strided_rows(bytes_f32, byte, MB * PATCHES).astype(BF16)
    value = mm_tn(x, dpp_ref[...])
    if not shards:
        refs[0][...] = value
        return
    total[...] = value
    store_shards(scal, total, refs[0], refs[1], None, order, 192, 4, pl.program_id(0))


def patch_weight_grad(scal, states, dpp, order, shards=True):
    if shards:
        out_shape = [sds((2, 4, 192, D), BF16)] * 2
        out_specs = [pl.BlockSpec((2, 1, 192, D), lambda i, s: (0, i ^ s[3], 0, 0))] * 2
    else:
        out_shape = [sds((PATCH // 2 * D, D), F32)]
        out_specs = [pl.BlockSpec((D, D), lambda i, s: (i, 0))]
    return pl.pallas_call(
        functools.partial(patch_grad_kernel, order=order, shards=shards),
        name="patch_weight_grad",
        out_shape=out_shape,
        grid_spec=pltpu.PrefetchScalarGridSpec(
            num_scalar_prefetch=1,
            grid=(PATCH // 2,),
            in_specs=[const_block(MB * SEQ, D), const_block(MB * PATCHES, D)],
            out_specs=out_specs,
            scratch_shapes=[pltpu.VMEM((LANES, MB * SEQ, 128), F32), pltpu.VMEM((D, D), F32)],
        ),
        compiler_params=pltpu.CompilerParams(vmem_limit_bytes=VLIMIT),
        cost_estimate=cost(1.2e9, 10e6),
    )(scal, states, dpp)


def input_grad_kernel(dpp_ref, dh_ref, wp_hbm, out_ref, acc, wp, psem):
    copies = [
        pltpu.make_async_copy(wp_hbm.at[pl.ds(j * D, D)], wp.at[pl.ds(j * D, D)], psem.at[j]) for j in range(PATCH)
    ]
    for copy in copies:
        copy.start()
    for j in range(PATCH):
        copies[j].wait()
        value = mm_nt(dpp_ref[...], wp[j * D : j * D + D, :])
        for b in range(LANES):
            acc[b, pl.ds(j, PATCHES, stride=PATCH), :] = value[:, b * 128 : b * 128 + 128]
    for b in range(LANES):
        cols = slice(b * 128, b * 128 + 128)
        out_ref[:, cols] = (dh_ref[:, cols] + acc[b]).astype(BF16)


def input_grad_part(dpp_own, dh, patch_weight):
    return pl.pallas_call(
        input_grad_kernel,
        name="input_grad",
        out_shape=sds((SEQ, D), BF16),
        in_specs=[pl.BlockSpec(memory_space=pltpu.VMEM)] * 2 + [ANY],
        out_specs=pl.BlockSpec(memory_space=pltpu.VMEM),
        scratch_shapes=[
            pltpu.VMEM((LANES, SEQ, 128), F32), pltpu.VMEM((PATCH * D, D), BF16), pltpu.SemaphoreType.DMA((PATCH,)),
        ],
        compiler_params=pltpu.CompilerParams(vmem_limit_bytes=VLIMIT),
        cost_estimate=cost(1.2e9, 15e6),
    )(dpp_own, dh, patch_weight)


class Job:
    def __init__(self, weight, lo, width, axes):
        self.weight, self.lo, self.width, self.axes = weight, lo, width, axes
        self.r = 192 if weight is None else ROWS_OF[weight]


class Alloc:
    def __init__(self):
        self.specs = []

    def __call__(self, shape, dtype):
        self.specs.append(pltpu.VMEM(shape, dtype))
        return len(self.specs) - 1


def store_unit(net, total, dst, r, axes, k_tile, cols, add):
    flip = lambda here, other: 1 - here if other else here
    for place in range(4 if k_tile is not None else 16):
        xr, yr = place % 2, place // 2 % 2
        k = place // 4 if k_tile is None else k_tile
        relative = {X: xr, Y: yr, ZN: k % 2, ZF: k // 2}
        shard = flip(net.y, yr) * 2 + flip(net.x, xr)
        if k_tile is None:
            shard = shard + 4 * (flip(net.z0, k % 2) + 2 * flip(net.z1, k // 2))
        index = 0
        for axis in axes:
            index = index * 2 + relative[axis]
        at_dst = (index,) if ZN in axes else (index, relative[ZN])
        at_dst += (slice(None), cols)
        value = total[pl.ds(pl.multiple_of(shard * r, 16), r), :]
        if add:
            value = value + dst[at_dst].astype(F32)
        dst[at_dst] = value.astype(BF16)


def job_buffers(alloc, job, local):
    block = (job.r, job.width) if ZN in job.axes else (2, job.r, job.width)
    count = 2 ** len(job.axes)
    job.own = alloc((count, *block), BF16)
    job.recv = []
    while count > 1:
        count //= 2
        job.recv.append(alloc((count, *block), BF16))
    if local:
        job.peer = alloc((16, *block), BF16)
        job.lf = alloc(block, F32)
        job.lr = alloc(block, F32)


def job_copies(net, b, job, local):
    job.copies = []
    count = 2 ** len(job.axes)
    for axis, recv in zip(job.axes, job.recv):
        job.copies.append(net.remote(b[job.own].at[count // 2 : count], b[recv], axis))
        count //= 2
    if local:
        job.cd = net.remote(b[job.peer], b[job.own], CORE)
        job.c4 = net.remote(b[job.lf], b[job.lr], CORE)


def advance(b, job, i):
    job.copies[i].wait_recv()
    own, recv = b[job.own], b[job.recv[i]]

    @pl.loop(0, 2 ** (len(job.axes) - 1 - i))
    def _(k):
        own[k] = add_low(own[k], recv[k])

    job.copies[i + 1].start()


def last_sum(b, job):
    job.copies[-1].wait_recv()
    return b[job.own][0].astype(F32) + b[job.recv[-1]][0].astype(F32)


def local_sum(net, b, job):
    b[job.lf][...] = last_sum(b, job)
    net.on(0, job.c4.start)


def stage_four(net, b, job, out):
    half = HALF_OF[job.weight]

    def finish():
        job.c4.wait_recv()
        out[:, job.lo : job.lo + job.width] = b[job.lr][...]
        out[:, half + job.lo : half + job.lo + job.width] = b[job.lf][...]

    net.on(1, finish)
    net.on(0, job.c4.wait_send)


def end_job(job):
    for copy in job.copies:
        copy.wait_send()


def local_products(net, b, jobs, mine, xt, total, x_ref, dy_ref):
    buffer = lambda job: b[job.own if mine else job.peer]
    job = jobs[0]
    base = (net.core if mine else 1 - net.core) * HALF_OF[job.weight] + job.lo
    if mine:
        for job in jobs:
            job.cd.wait_recv()
    if job.weight == DOWN:

        @pl.loop(0, 4)
        def _(k):
            xt[...] = x_ref[:, lanes(net.z_of(k) * D, D)].T
            total[...] = mm(xt[...], dy_ref[:, lanes(base, UNIT)])
            for job in jobs:
                part = total.at[:, job.lo : job.lo + job.width]
                store_unit(net, part, buffer(job), job.r, job.axes, k, slice(0, job.width), mine)
    else:
        if x_ref is not None:
            xt[...] = x_ref[...].T

        @pl.loop(0, job.width // UNIT)
        def _(n):
            total[...] = mm(xt[...], dy_ref[:, lanes(base + n * UNIT, UNIT)])
            store_unit(net, total, buffer(job), job.r, job.axes, None, lanes(n * UNIT, UNIT), mine)

    for job in jobs:
        if mine:
            job.copies[0].start()
            job.cd.wait_send()
        else:
            job.cd.start()


def first_plan():
    alloc = Alloc()
    jobs = [
        Job(DOWN, 0, 256, (X, Y, ZN, ZF)), Job(DOWN, 256, 128, (Y, X, ZN, ZF)),
        Job(UP, 0, 768, (X, Y, ZN, ZF)), Job(UP, 768, 768, (X, Y, ZN, ZF)),
    ]
    for job in jobs:
        job_buffers(alloc, job, True)
    s = lambda: None
    s.jobs = jobs
    s.ubuf, s.dz = alloc((SEQ, FF), BF16), alloc((SEQ, FF), BF16)
    s.dm = alloc((SEQ, D), BF16)
    s.xt, s.total = alloc((D, SEQ), BF16), alloc((D, UNIT), F32)
    s.wq, s.wo, s.wu, s.wd = (alloc(w, BF16) for w in ((D, 3 * D), (D, D), (D, FF), (FF, D)))
    s.gp = alloc((2, TILE, FF), BF16)
    s.bytes, s.mid = alloc((2, TILE, D), BF16), alloc((2, TILE, D), F32)
    s.qkv, s.p = alloc((2, TILE, 3 * D), BF16), alloc((2, SUBS, PAIRS, 256, 128), BF16)
    s.dr, s.dqkv, s.dh, s.do = alloc((TILE, D), BF16), alloc((TILE, 3 * D), BF16), alloc((TILE, D), F32), alloc((TILE, D), BF16)
    s.g, s.dg, s.dmg, s.dpp = (alloc((n, D), BF16) for n in (PATCHES, PATCHES, ROWS_G, ROWS_G))
    s.gains = alloc((2, 2, D), F32)
    s.specs = alloc.specs
    return s


def first_kernel(
    u_in, dm_in, c_in, gp_in, states, g_in, mid_in, qkv_in, p_in, gains_own, gains_other,
    wq_own, wo_own, wu_own, wd_own, wq_other, wo_other, wu_other, wd_other,
    start_g, mid_g, qkv_g, p_g, gp_g, pat_in, xg_in,
    out_up, out_down, dr_out, dqkv_out, dh_out, dpp_out, keep_out, send_out, pat_out, xn_out, gain_out,
    *refs, plan,
):
    b, (load_sem, tile_sem, send_sem, recv_sem) = refs[:-4], refs[-4:]
    net = Net(send_sem, recv_sem, load_sem)
    s = plan
    core = net.core
    down0, down1, up0, up1 = s.jobs
    net.meet()
    for job in s.jobs:
        job_copies(net, b, job, True)
    dg_copy = net.remote(b[s.dg], b[s.dmg].at[PATCHES:ROWS_G, :], CORE)
    pat_copies = [net.remote(pat_in.at[i], pat_out.at[i - 1], to) for i, to in ((1, X), (2, Y), (3, XY))]
    xg_copy = net.remote(xg_in, xn_out, ZN)
    net.on(0, xg_copy.start)

    def load(src, dst):
        copy = net.load(src, dst)
        copy.start()
        return copy

    def load_weight(own, other, dst, swap):
        copy = net.load(own.at[0], dst)
        net.on(0 if swap else 1, copy.start)
        if not swap:
            second = net.load(other.at[0], dst)
            net.on(0, second.start)

        def wait():
            if swap:
                net.on(0, copy.wait)
            else:
                net.on(1, copy.wait)
                net.on(0, second.wait)

        return wait

    u_load, dm_load = load(u_in, b[s.ubuf]), load(dm_in, b[s.dm])
    wd_wait = load_weight(wd_own, wd_other, b[s.wd], False)
    small = [load(g_in, b[s.g]), load(gains_own.at[0], b[s.gains].at[0]), load(gains_other.at[0], b[s.gains].at[1])]
    wu_wait = load_weight(wu_own, wu_other, b[s.wu], False)
    wo_wait = load_weight(wo_own, wo_other, b[s.wo], False)
    wq_wait = load_weight(wq_own, wq_other, b[s.wq], False)

    def tile_copies(t, slot, kinds):
        rows = pl.ds(pl.multiple_of(t * TILE, TILE), TILE)
        seq_rows = pl.ds(pl.multiple_of(core * SEQ + t * TILE, TILE), TILE)
        subs = pl.ds(t * SUBS, SUBS)
        table = (
            (gp_in.at[rows, :], b[s.gp].at[slot]), (states.at[seq_rows, :], b[s.bytes].at[slot]),
            (mid_in.at[rows, :], b[s.mid].at[slot]), (qkv_in.at[rows, :], b[s.qkv].at[slot]),
            (p_in.at[subs], b[s.p].at[slot]),
        )
        return [pltpu.make_async_copy(*table[i], tile_sem.at[slot, i]) for i in kinds]

    def store_copies(t):
        rows = pl.ds(pl.multiple_of(t * TILE, TILE), TILE)
        table = ((b[s.dr], dr_out), (b[s.dqkv], dqkv_out), (b[s.dh], dh_out))
        return [pltpu.make_async_copy(src, dst.at[rows, :], tile_sem.at[2, i]) for i, (src, dst) in enumerate(table)]

    for copy in tile_copies(0, 0, (0, 1, 2, 3, 4)):
        copy.start()
    u_load.wait()
    dm_load.wait()
    xt, total = b[s.xt], b[s.total]

    def dz_tiles(first, last):
        @pl.loop(first, last)
        def _(t):
            slot = t % 2
            tile_copies(t, slot, (0,))[0].wait()

            @pl.when(t + 1 < TILES)
            def _():
                tile_copies(t + 1, 1 - slot, (0,))[0].start()

            rows = pl.ds(pl.multiple_of(t * TILE, TILE), TILE)
            dz_product(b[s.dm][rows, :], b[s.wd], b[s.gp].at[slot], b[s.dz].at[rows, :])

    local_products(net, b, [down0, down1], False, xt, total, b[s.ubuf], b[s.dm])
    wd_wait()
    dz_tiles(0, 2)
    local_products(net, b, [down0, down1], True, xt, total, b[s.ubuf], b[s.dm])
    c_part = b[s.ubuf].at[:, 0:D]
    c_load = load(c_in, c_part)
    dz_tiles(2, TILES)
    wd_wait_g = load_weight(wd_own, wd_other, b[s.wd], True)
    c_load.wait()
    local_products(net, b, [up0], False, xt, total, c_part, b[s.dz])
    local_products(net, b, [up1], False, xt, total, None, b[s.dz])
    advance(b, down1, 0)
    local_products(net, b, [up0], True, xt, total, None, b[s.dz])
    local_products(net, b, [up1], True, xt, total, None, b[s.dz])
    for copy in small:
        copy.wait()
    wu_wait()
    wo_wait()
    wq_wait()
    gains = jnp.where(core == 1, b[s.gains][0], b[s.gains][1])
    gain_out[...] = jnp.zeros_like(gain_out)

    def global_loads():
        pairs = (
            (gp_g, b[s.gp].at[0]), (mid_g, b[s.mid].at[0]), (qkv_g, b[s.qkv].at[0]), (p_g, b[s.p].at[0]),
        )
        return [pltpu.make_async_copy(*pair, tile_sem.at[3, i]) for i, pair in enumerate(pairs)]

    @pl.loop(0, TILES)
    def _(t):
        slot = t % 2
        for copy in tile_copies(t, slot, (1, 2, 3, 4)):
            copy.wait()

        @pl.when(t + 1 < TILES)
        def _():
            for copy in tile_copies(t + 1, 1 - slot, (1, 2, 3, 4)):
                copy.start()

        @pl.when((t + 1 == TILES) & (core == 0))
        def _():
            for copy in global_loads():
                copy.start()

        @pl.when(t > 0)
        def _():
            for copy in store_copies(t - 1):
                copy.wait()

        rows = pl.ds(pl.multiple_of(t * TILE, TILE), TILE)
        patch_rows = pl.ds(pl.multiple_of(t * (TILE // PATCH), TILE // PATCH), TILE // PATCH)
        h = b[s.bytes][slot].astype(F32) + mm(spread_matrix(), b[s.g][patch_rows, :])
        dh, dgain = block_backward(
            b[s.dm][rows, :].astype(F32), h, gains, (b[s.wq], b[s.wo], b[s.wu]), lambda i: None,
            b[s.dz].at[rows, :], b[s.mid].at[slot], b[s.qkv].at[slot], b[s.p].at[slot], b[s.do], b[s.dr], b[s.dqkv],
            b[s.dh],
        )
        b[s.dh][...] = dh
        b[s.dg][patch_rows, :] = jnp.sum(dh.reshape(TILE // PATCH, PATCH, D), axis=1).astype(BF16)
        gain_out[2:4, :] += dgain
        for copy in store_copies(t):
            copy.start()

        @pl.when(t == 0)
        def _():
            advance(b, down1, 1)
            advance(b, down0, 0)

        @pl.when(t == 1)
        def _():
            for copy in pat_copies:
                copy.start()
            advance(b, down1, 2)

        @pl.when(t == 2)
        def _():
            local_sum(net, b, down1)
            advance(b, down0, 1)
            advance(b, up0, 0)

        @pl.when(t == 3)
        def _():
            advance(b, down0, 2)
            advance(b, up0, 1)
            advance(b, up1, 0)

    wu_wait_g = load_weight(wu_own, wu_other, b[s.wu], True)
    wo_wait_g = load_weight(wo_own, wo_other, b[s.wo], True)
    wq_wait_g = load_weight(wq_own, wq_other, b[s.wq], True)
    net.on(1, dg_copy.start)
    for copy in store_copies(TILES - 1):
        copy.wait()
    dz_g = b[s.ubuf].at[0:ROWS_G, :]
    wd_wait_g()
    wu_wait_g()
    wo_wait_g()
    wq_wait_g()

    start_load = pltpu.make_async_copy(start_g, b[s.mid].at[1], tile_sem.at[3, 4])

    def global_upper():
        start_load.start()
        for copy in global_loads():
            copy.wait()
        b[s.dmg][0:PATCHES, :] = b[s.dg][...]
        dg_copy.wait_recv()
        dz_product(b[s.dmg][...], b[s.wd], b[s.gp].at[0], dz_g)
        gain_out[1:2, :] = backward_upper(
            b[s.dmg][...].astype(F32), b[s.gains][0], b[s.wo], b[s.wu], dz_g, b[s.mid].at[0], b[s.dr], b[s.do], b[s.dh]
        )

    def global_lower():
        start_load.wait()
        dh, dgain = backward_lower(
            b[s.mid][1], b[s.gains][0], b[s.wq], b[s.qkv].at[0], b[s.p].at[0], b[s.do], b[s.dqkv], b[s.dh]
        )
        gain_out[0:1, :] = dgain
        moved = pltpu.roll(dh, ROWS_G - 1, 0)
        row = lax.broadcasted_iota(jnp.int32, (ROWS_G, D), 0)
        b[s.dpp][...] = jnp.where((row & (PATCHES - 1)) == PATCHES - 1, 0.0, moved).astype(BF16)
        for copy in global_stores():
            copy.start()

    def global_stores():
        copies = [pltpu.make_async_copy(b[s.dpp], dpp_out, tile_sem.at[4, 0])]
        lo, n = 0, 1
        for src, width in ((b[s.dqkv], 3 * D // 2), (b[s.dr], D // 2), (dz_g, FF // 2), (b[s.dmg], D // 2)):
            for out, half in ((keep_out, net.z0), (send_out, 1 - net.z0)):
                copies.append(
                    pltpu.make_async_copy(src.at[:, lanes(half * width, width)], out.at[:, lo : lo + width], tile_sem.at[4, n])
                )
                n += 1
            lo += width
        return copies

    net.on(0, global_upper)
    local_sum(net, b, down0)
    advance(b, up0, 2)
    advance(b, up1, 1)
    net.on(0, global_lower)
    stage_four(net, b, down1, out_down)
    stage_four(net, b, down0, out_down)
    local_sum(net, b, up0)
    advance(b, up1, 2)
    stage_four(net, b, up0, out_up)
    local_sum(net, b, up1)
    net.on(1, dg_copy.wait_send)
    stage_four(net, b, up1, out_up)
    for job in s.jobs:
        end_job(job)
    for copy in pat_copies:
        copy.wait()
    net.on(0, xg_copy.wait)

    def finish():
        for copy in global_stores():
            copy.wait()

    net.on(0, finish)


def first_part(u, dm, c, gp, states, g, mid, qkv, p, gains, gains_other, weights, other, saved, pat, xg):
    plan = first_plan()
    outs = [
        ((D // 16, FF), F32), ((FF // 16, D), F32), ((SEQ, D), BF16), ((SEQ, 3 * D), BF16), ((SEQ, D), F32),
        ((ROWS_G, D), BF16), ((ROWS_G, WIDTH_G), BF16), ((ROWS_G, WIDTH_G), BF16), ((3, PATCH // 2, ROWS_G, 192), BF16), ((ROWS_G, XG), BF16),
        ((8, D), F32),
    ]
    vmem = pl.BlockSpec(memory_space=pltpu.VMEM)
    operands = (u, dm, c, gp, states, g, mid, qkv, p, gains, gains_other, *weights, *other, *saved, pat, xg)
    return pl.pallas_call(
        functools.partial(first_kernel, plan=plan),
        name="first_part",
        out_shape=[sds(*o) for o in outs],
        in_specs=[ANY] * len(operands),
        out_specs=[vmem] * 2 + [ANY] * 8 + [vmem],
        scratch_shapes=plan.specs + [
            pltpu.SemaphoreType.DMA((32,)), pltpu.SemaphoreType.DMA((5, 9)), pltpu.SemaphoreType.DMA((40,)),
            pltpu.SemaphoreType.DMA((40,)),
        ],
        compiler_params=pltpu.CompilerParams(vmem_limit_bytes=63 * 2**20, collective_id=1, has_side_effects=True),
        cost_estimate=cost(35e9, 80e6),
    )(*operands)


def second_plan():
    alloc = Alloc()
    s = lambda: None
    s.local = [Job(QKV, 0, 768, (X, Y, ZN, ZF)), Job(QKV, 768, 384, (X, Y, ZN, ZF)), Job(OUT, 0, 384, (Y, X, ZN, ZF))]
    s.patch = Job(None, 0, D, (ZN, ZF))
    s.glob = [
        Job(DOWN, 0, 384, (Y, X, ZF)), Job(UP, 0, 768, (X, Y, ZF)), Job(UP, 768, 768, (Y, X, ZF)),
        Job(QKV, 0, 768, (Y, X, ZF)), Job(QKV, 768, 384, (Y, X, ZF)), Job(OUT, 0, 384, (Y, X, ZF)),
    ]
    for job in s.local:
        job_buffers(alloc, job, True)
    job_buffers(alloc, s.patch, False)
    for job in s.glob:
        job_buffers(alloc, job, False)
        job.swap = alloc((2, job.r, job.width), BF16)
    s.dqkv = alloc((SEQ, 3 * D), BF16)
    s.a, s.o, s.dr = (alloc((SEQ, D), BF16) for _ in range(3))
    s.xt, s.xo, s.total = alloc((D, SEQ), BF16), alloc((D, SEQ), BF16), alloc((D, UNIT), F32)
    s.pat, s.dpp = alloc((PATCH // 2, 4 * ROWS_G, 192), BF16), alloc((4 * ROWS_G, D), BF16)
    s.xg, s.dy = alloc((2 * ROWS_G, XG), BF16), alloc((2 * ROWS_G, WIDTH_G), BF16)
    s.gains = alloc((6, 8, D), F32)
    s.g, s.spread = alloc((ROWS_G, D), BF16), alloc((2, TILE, D), BF16)
    s.wp, s.acc = alloc((2, D, D), BF16), alloc((LANES, SEQ, 128), F32)
    s.specs = alloc.specs
    return s


def second_kernel(
    pat_own, pat_in, dpp_in, o_in, dr_in, a_in, dqkv_in, xg_in, xn_in, keep_in, send_in, dh_in, wp_in, g_in, y_in,
    gains_in, up_in, down_in,
    out_qkv, out_out, out_up, out_down, out_patch, out_gains, out_mine, out_peer, out_rows, *refs, plan,
):
    b, (load_sem, wp_sem, row_sem, send_sem, recv_sem) = refs[:-5], refs[-5:]
    net = Net(send_sem, recv_sem, load_sem)
    s = plan
    core = net.core
    q0, q1, proj = s.local
    outs = (out_qkv, out_out, out_up, out_down)
    net.meet()
    for job in s.local:
        job_copies(net, b, job, True)
    job_copies(net, b, s.patch, False)
    for job in s.glob:
        job_copies(net, b, job, False)
        job.swap_copy = net.remote(b[job.swap].at[0], b[job.swap].at[1], ZN)
    gain_copies = [
        net.remote(b[s.gains].at[0], b[s.gains].at[i + 1], to) for i, to in enumerate((CORE, X, Y, ZN, ZF))
    ]
    dpp_slots = [b[s.dpp].at[i * ROWS_G : i * ROWS_G + ROWS_G, :] for i in range(4)]
    dpp_gives = [net.remote(dpp_in, dpp_slots[0], CORE)] + [net.remote(slot, slot, CORE) for slot in dpp_slots[1:]]
    dpp_copies = [net.remote(dpp_in, dpp_slots[i], to) for i, to in ((1, X), (2, Y), (3, XY))]
    own_part, next_part = slice(0, ROWS_G), slice(ROWS_G, 2 * ROWS_G)
    dyn_copy = net.remote(send_in, b[s.dy].at[next_part, :], ZN)
    grad_copy = net.remote(out_mine, out_peer, CORE)
    y_copy = net.remote(y_in, out_rows.at[0:SEQ, :], CORE)
    y_own = net.load(y_in, out_rows.at[SEQ : MB * SEQ, :])
    g_load = net.load(g_in, b[s.g])
    dpp_load = net.load(dpp_in, dpp_slots[0])
    global_copies = [net.load(*pair) for pair in (
        (xg_in, b[s.xg].at[own_part, :]), (xn_in, b[s.xg].at[next_part, :]), (keep_in, b[s.dy].at[own_part, :]),
    )]

    def give():
        dpp_gives[0].start()
        for copy in dpp_copies:
            copy.start()
        dyn_copy.start()
        dpp_load.start()
        g_load.start()
        y_copy.start()

    net.on(0, give)
    net.on(1, y_own.start)
    rest = [net.load(*pair) for pair in ((dqkv_in, b[s.dqkv]), (a_in, b[s.a]), (o_in, b[s.o]), (dr_in, b[s.dr]))]
    pat_parts = [pat_own.at[0]] + [pat_in.at[i] for i in range(3)]
    pat_loads = [
        net.load(part, b[s.pat].at[:, i * ROWS_G : i * ROWS_G + ROWS_G, :]) for i, part in enumerate(pat_parts)
    ]
    gain_load = net.load(gains_in, b[s.gains].at[0])
    dh_loads = [net.load(dh_in.at[:, i * 128 : i * 128 + 128], b[s.acc].at[i]) for i in range(LANES)]
    for copy in rest + [gain_load] + pat_loads + dh_loads:
        copy.start()
    net.on(0, lambda: [copy.start() for copy in global_copies] and None)

    def gain_step(i):
        if i == 0:
            gain_load.wait()
        else:
            gain_copies[i - 1].wait_recv()
            b[s.gains][0] = b[s.gains][0] + b[s.gains][i]
        if i < 5:
            gain_copies[i].start()
            gain_copies[i].wait_send()

    def forward_dpp():
        def work():
            for copy, give_copy in zip(dpp_copies, dpp_gives[1:]):
                copy.wait_recv()
                give_copy.start()

        net.on(0, work)

    def patch_products(job):
        for copy in pat_loads:
            copy.wait()
        for i in range(PATCH // 2):
            b[s.xt][i * 192 : i * 192 + 192, :] = b[s.pat][i].T
        net.on(1, lambda: [copy.wait_recv() for copy in dpp_gives[1:]] and None)

        @pl.loop(0, D // UNIT)
        def _(n):
            cols = lanes(n * UNIT, UNIT)
            b[s.total][...] = mm(b[s.xt][...], b[s.dpp][:, cols])
            for k in range(4):
                z = (1 - net.z0 if k // 2 else net.z0) + 2 * (1 - net.z1 if k % 2 else net.z1)
                b[job.own][k, :, cols] = b[s.total][pl.ds(pl.multiple_of(z * 192, 16), 192), :].astype(BF16)
        job.copies[0].start()

    def global_products(job):
        base = DY_LO[job.weight] + job.lo

        def product(cols, n):
            return mm_tn(b[s.xg][:, cols], b[s.dy][:, lanes(base + n * UNIT, UNIT)])

        def work():
            if job.weight == DOWN:

                @pl.loop(0, 4)
                def _(k):
                    b[s.total][...] = product(lanes(X_LO[DOWN] + net.z_of(k) * D, D), 0)
                    store_unit(net, b[s.total], b[job.own], job.r, job.axes, k, slice(0, UNIT), False)
            else:

                @pl.loop(0, job.width // UNIT)
                def _(n):
                    b[s.total][...] = product(slice(X_LO[job.weight], X_LO[job.weight] + D), n)
                    store_unit(net, b[s.total], b[job.own], job.r, job.axes, None, lanes(n * UNIT, UNIT), False)

            job.copies[0].start()

        net.on(0, work)

    def global_advance(job, i):
        net.on(0, lambda: advance(b, job, i))

    def global_sum(job):
        def work():
            value = last_sum(b, job)
            b[job.swap][0] = value[1].astype(BF16)
            job.swap_copy.start()
            outs[job.weight][:, lanes(net.z0 * HALF_OF[job.weight] + job.lo, job.width)] = value[0]

        net.on(0, work)

    def global_end(job):
        def work():
            job.swap_copy.wait_recv()
            cols = lanes((1 - net.z0) * HALF_OF[job.weight] + job.lo, job.width)
            outs[job.weight][:, cols] = b[job.swap][1].astype(F32)

        net.on(0, work)

    def wp_copy(j):
        slot = j % 2
        rows = pl.ds(pl.multiple_of(j * D, D), D)
        return pltpu.make_async_copy(wp_in.at[rows, :], b[s.wp].at[slot], wp_sem.at[slot])

    def input_grads():
        own = pl.ds(pl.multiple_of(core * PATCHES, PATCHES), PATCHES)
        for copy in dh_loads:
            copy.wait()

        @pl.loop(0, PATCH)
        def _(j):
            wp_copy(j).wait()

            @pl.when(j + 1 < PATCH)
            def _():
                wp_copy(j + 1).start()

            value = mm_nt(b[s.dpp][own, :], b[s.wp][j % 2])
            for i in range(LANES):
                places = (i, pl.ds(j, PATCHES, stride=PATCH), slice(None))
                b[s.acc][places] = b[s.acc][places] + value[:, i * 128 : i * 128 + 128]

        for i in range(LANES):
            out_mine[:, i * 128 : i * 128 + 128] = b[s.acc][i].astype(BF16)
        grad_copy.start()

    def first_wait():
        for copy in global_copies:
            copy.wait()
        dyn_copy.wait_recv()

    def spread_copy(i):
        return pltpu.make_async_copy(
            b[s.spread].at[i % 2], out_rows.at[pl.ds(pl.multiple_of(i * TILE, TILE), TILE), :], row_sem.at[i % 2]
        )

    def spread_rows():
        g_load.wait()
        matrix = spread_matrix()

        @pl.loop(0, MB * TILES)
        def _(i):
            @pl.when(i >= 2)
            def _():
                spread_copy(i - 2).wait()

            rows = pl.ds(pl.multiple_of(i * (TILE // PATCH), TILE // PATCH), TILE // PATCH)
            b[s.spread][i % 2] = mm(matrix, b[s.g][rows, :]).astype(BF16)
            spread_copy(i).start()

        for i in (MB * TILES - 2, MB * TILES - 1):
            spread_copy(i).wait()

    wp_copy(0).start()
    g_down, g_up0, g_up1, g_q0, g_q1, g_out = s.glob
    patch = s.patch
    for copy in rest:
        copy.wait()
    xt, xo, total = b[s.xt], b[s.xo], b[s.total]
    local_products(net, b, [q0], False, xt, total, b[s.a], b[s.dqkv])
    local_products(net, b, [q1], False, xt, total, None, b[s.dqkv])
    local_products(net, b, [proj], False, xo, total, b[s.o], b[s.dr])
    gain_step(0)
    net.on(0, dpp_load.wait)
    net.on(1, dpp_gives[0].wait_recv)
    input_grads()
    gain_step(1)
    forward_dpp()
    local_products(net, b, [q0], True, xt, total, None, b[s.dqkv])
    local_products(net, b, [q1], True, xt, total, None, b[s.dqkv])
    local_products(net, b, [proj], True, xo, total, None, b[s.dr])
    net.on(0, first_wait)
    gain_step(2)
    global_products(g_down)
    patch_products(patch)
    global_products(g_up0)
    advance(b, proj, 0)
    global_products(g_up1)
    advance(b, q0, 0)
    global_products(g_q0)
    global_products(g_q1)
    global_products(g_out)
    net.on(0, spread_rows)
    gain_step(3)
    advance(b, q1, 0)
    global_advance(g_down, 0)
    advance(b, patch, 0)
    global_advance(g_up0, 0)
    gain_step(4)
    global_advance(g_up1, 0)
    advance(b, proj, 1)
    advance(b, proj, 2)
    advance(b, q0, 1)
    global_advance(g_down, 1)
    gain_step(5)
    out_patch[...] = last_sum(b, patch)
    out_gains[...] = b[s.gains][0]

    def copy_first():
        out_up[...] = up_in[...]
        out_down[...] = down_in[...]

    net.on(1, copy_first)
    global_advance(g_up1, 1)
    local_sum(net, b, proj)
    global_advance(g_q0, 0)
    stage_four(net, b, proj, out_out)
    advance(b, q0, 2)
    global_advance(g_q1, 0)
    global_sum(g_down)
    global_advance(g_q0, 1)
    global_advance(g_out, 0)
    global_advance(g_q1, 1)
    global_sum(g_up1)
    advance(b, q1, 1)
    global_advance(g_out, 1)
    local_sum(net, b, q0)
    global_end(g_down)
    global_advance(g_up0, 1)
    stage_four(net, b, q0, out_qkv)
    global_sum(g_q0)
    global_end(g_up1)
    global_sum(g_q1)
    advance(b, q1, 2)
    global_sum(g_out)
    global_sum(g_up0)
    global_end(g_q0)
    global_end(g_q1)
    local_sum(net, b, q1)
    global_end(g_out)
    global_end(g_up0)
    stage_four(net, b, q1, out_qkv)
    for job in s.local + [patch]:
        end_job(job)
    grad_copy.wait()

    def end_rows():
        y_own.wait()
        y_copy.wait_recv()

    net.on(1, end_rows)

    def drain():
        for copy in dpp_gives + dpp_copies + [dyn_copy, y_copy]:
            copy.wait_send()
        for job in s.glob:
            end_job(job)
            job.swap_copy.wait_send()

    net.on(0, drain)


def second_part(*operands):
    plan = second_plan()
    outs = [((ROWS_OF[w], 2 * HALF_OF[w]), F32) for w in (QKV, OUT, UP, DOWN)] + [((192, D), F32), ((8, D), F32)]
    outs += [((SEQ, D), BF16)] * 2 + [((MB * SEQ, D), BF16)]
    vmem = pl.BlockSpec(memory_space=pltpu.VMEM)
    return pl.pallas_call(
        functools.partial(second_kernel, plan=plan),
        name="second_part",
        out_shape=[sds(*o) for o in outs],
        in_specs=[ANY] * (len(operands) - 2) + [vmem] * 2,
        out_specs=[vmem] * (len(outs) - 1) + [ANY],
        scratch_shapes=plan.specs + [
            pltpu.SemaphoreType.DMA((24,)), pltpu.SemaphoreType.DMA((2,)), pltpu.SemaphoreType.DMA((2,)),
            pltpu.SemaphoreType.DMA((64,)), pltpu.SemaphoreType.DMA((64,)),
        ],
        compiler_params=pltpu.CompilerParams(vmem_limit_bytes=63 * 2**20, collective_id=2, has_side_effects=True),
        cost_estimate=cost(15e9, 60e6),
    )(*operands)


def finish_kernel(*refs):
    own, peer = refs[:2]
    sources, grad_out = refs[2:8], refs[8]
    targets, refs = refs[9:15], refs[15:]
    held, wide, staged = refs[0], refs[1], refs[2:8]
    copy_sem, in_sem, out_sem = refs[8:]
    core = lax.axis_index("section")
    loads = [pltpu.make_async_copy(src, held.at[i], in_sem.at[i]) for i, src in enumerate((own, peer))]
    copies_in = [pltpu.make_async_copy(src, mid, copy_sem.at[0, i]) for i, (src, mid) in enumerate(zip(sources, staged))]
    copies_out = [pltpu.make_async_copy(mid, dst, copy_sem.at[1, i]) for i, (mid, dst) in enumerate(zip(staged, targets))]
    for copy in loads + copies_in:
        copy.start()

    def store(i, t):
        place = core if i == 0 else 1 - core
        rows = pl.ds(pl.multiple_of(place * SEQ + t * TILE, TILE), TILE)
        return pltpu.make_async_copy(wide.at[i * TILES + t], grad_out.at[rows, :], out_sem.at[i * TILES + t])

    for i in range(2):
        loads[i].wait()

        @pl.loop(0, TILES)
        def _(t, i=i):
            wide[i * TILES + t] = held[i, pl.ds(pl.multiple_of(t * TILE, TILE), TILE), :].astype(F32)
            store(i, t).start()

    for first, second in zip(copies_in, copies_out):
        first.wait()
        second.start()
    for i in range(2):
        @pl.loop(0, TILES)
        def _(t, i=i):
            store(i, t).wait()

    for copy in copies_out:
        copy.wait()


def finish(own_grad, peer_grad, others):
    outs = [((MB * SEQ, D), F32)] + [(v.shape, v.dtype) for v in others]
    return pl.pallas_call(
        finish_kernel,
        name="finish",
        out_shape=[sds(*o) for o in outs],
        in_specs=[ANY] * (2 + len(others)),
        out_specs=[ANY] * len(outs),
        scratch_shapes=[
            pltpu.VMEM((2, SEQ, D), BF16), pltpu.VMEM((2 * TILES, TILE, D), F32),
            *[pltpu.VMEM(v.shape, v.dtype) for v in others], pltpu.SemaphoreType.DMA((2, len(others))),
            pltpu.SemaphoreType.DMA((2,)), pltpu.SemaphoreType.DMA((2 * TILES,)),
        ],
        compiler_params=pltpu.CompilerParams(vmem_limit_bytes=VLIMIT),
        cost_estimate=cost(1e6, 20e6),
    )(own_grad, peer_grad, *others)


def swap_core(value):
    return lax.ppermute(value, "section", [(0, 1), (1, 0)])


def hop(value, mask, cores):
    size = lax.axis_size("dp")
    if cores == (0, 1):
        return lax.ppermute(value, "dp", [(i, i ^ mask) for i in range(size)])
    pairs = [(c * size + i, c * size + (i ^ mask)) for c in cores for i in range(size)]
    return lax.ppermute(value, ("section", "dp"), pairs)


HOPS = {"x": 1, "y": 2}


def body(states, lengths, patch_weight, w_qkv, w_out, w_up, w_down, gains, cotangent):
    size = lax.axis_size("dp")
    fast = size == 16
    core = lax.axis_index("section")
    at = lax.axis_index("dp")
    mx, my, mz = at % 2, (at // 2) % 2, (at // 4) % 4
    length = jnp.where(core == 0, lengths[0], lengths[1])
    scal = jnp.stack([core, mx, my, mz, length]).astype(jnp.int32)
    weights = (w_qkv, w_out, w_up, w_down)
    other = tuple(swap_core(w) for w in weights)
    gains_other = swap_core(gains)

    g_own, g_all, xg, start, qkv_g, p_g, mid_g, gp_g, pat = global_forward(states, gains, patch_weight, weights)
    y, dm, a, qkv, p, o, mid, c, u, gp = local_forward(
        scal, states, cotangent, g_own, gains, weights, gains_other, other
    )
    saved = (start, mid_g, qkv_g, p_g, gp_g)
    if fast:
        up_l, down_l, dr, dqkv, dh, dpp, dy_keep, dy_send, pat_next, xg_next, gain_parts = first_part(
            u, dm, c, gp, states, g_own, mid, qkv, p, gains, gains_other, weights, other, saved, pat, xg
        )
        *grads, patch_grad, gain_sums, own_grad, peer_grad, section_rows = second_part(
            pat, pat_next, dpp, o, dr, a, dqkv, xg, xg_next, dy_keep, dy_send, dh, patch_weight, g_all, y,
            gain_parts, up_l, down_l
        )
        input_grad, section_rows, patch_grad, *grads = finish(own_grad, peer_grad, (section_rows, patch_grad, *grads))
        outs = tuple(g[None] for g in grads)
    else:
        dz = local_dz(scal, dm, gp, w_down, other[3])
        dr, dqkv, dh, dg, dgain_l = local_backward(
            scal, dz, dm, states, g_own, mid, qkv, p, gains, weights[:3], gains_other, other[:3]
        )
        dpp, dy_keep, dy_send, dgain_g = global_backward(scal, (dg, swap_core(dg)), saved, gains, weights)
        gain_parts = jnp.concatenate([dgain_g[:2], dgain_l[:2], jnp.zeros((4, D), F32)], axis=0)
        dpp = jnp.where(core == 0, dpp, swap_core(dpp))
        own_grad = input_grad_part(jnp.where(core == 0, dpp[:PATCHES], dpp[PATCHES:]), dh, patch_weight)
        peer_grad = swap_core(own_grad)
        input_grad = jnp.where(
            core == 0, jnp.concatenate([own_grad, peer_grad]), jnp.concatenate([peer_grad, own_grad])
        ).astype(F32)
        g_rows = jnp.broadcast_to(g_all[:, None, :], (MB * PATCHES, PATCH, D)).reshape(MB * SEQ, D)
        section_rows = jnp.where(core == 0, g_rows, jnp.concatenate([swap_core(y), y], axis=0))
        gain_sums = lax.psum(gain_parts, ("section", "dp"))
        (patch_half,) = patch_weight_grad(scal, states, dpp, "xy", shards=False)
        patch_grad = lax.psum_scatter(patch_half, "dp", scatter_dimension=0, tiled=True)
        half = D // 2
        swap_halves = lambda keep, send, lo, width: jnp.where(
            mx == 0,
            jnp.concatenate([keep[:, lo : lo + width], send[:, lo : lo + width]], axis=1),
            jnp.concatenate([send[:, lo : lo + width], keep[:, lo : lo + width]], axis=1),
        )

        def whole_grad(x_lo, dy_lo, x, dy, rows, cols):
            dy_g = swap_halves(dy_keep, dy_send, dy_lo, cols // 2)
            glob = weight_grad(scal, [xg], x_lo, [dy_g], 0, rows, cols, 384, "xy", shards=False)
            loc = weight_grad(scal, [x], 0, [dy], 0, rows, cols, 384, "xy", shards=False)
            total = jnp.where(core == 0, glob, loc + swap_core(loc))
            return lax.psum_scatter(total, "dp", scatter_dimension=0, tiled=True)[None]

        outs = (
            whole_grad(0, 0, a, dqkv, D, 3 * D),
            whole_grad(D, 3 * half, o, dr, D, D),
            whole_grad(2 * D, 4 * half, c, dz, D, FF),
            whole_grad(3 * D, 8 * half, u, dm, FF, D),
        )
    share = D // size
    own_gains = jnp.where(core == 0, gain_sums[0:2], gain_sums[2:4])
    gain_grad = lax.dynamic_slice(own_gains, (0, at * share), (2, share))
    return (section_rows[None], input_grad, patch_grad, *outs, gain_grad[None])


def solution(mesh):
    return jax.shard_map(
        body,
        mesh=mesh,
        in_specs=(
            P("dp", None), P("dp"), P(), P("section", None, None), P("section", None, None),
            P("section", None, None), P("section", None, None), P("section", None, None), P("dp", None),
        ),
        out_specs=(
            P("section", "dp", None), P("dp", None), P(("section", "dp"), None), P("section", "dp", None),
            P("section", "dp", None), P("section", "dp", None), P("section", "dp", None), P("section", None, "dp"),
        ),
        check_vma=False,
    )
```

profile of v0, /device:TPU:8, one launch (start us, length us, event | category | flops | bytes accessed | tf_op | source)
XLA Modules:
  0.0 269.6 jit_solution(4096213787366340204)
XLA Ops:
  0.6 0.0 copy-start
  0.6 0.1 collective-permute-start.2
  0.7 0.5 collective-permute-start.3
  1.2 0.1 collective-permute-start
  1.3 0.4 collective-permute-start.1
  1.7 0.1 collective-permute-start.4
  1.8 19.2 %global_forward.1 = (bf16[128,768]{1,0:T(8,128)(2,1)}, bf16[256,768]{1,0:T(8,128)(2,1)}, bf16[256,5376]{1,0:T(8,128)(2,1)}, f32[256,768]{1,0:T(8,128)}, bf16[256...) custom-call(bf16[2048,768]{1,0:T(8,128)(2,1)} %states.1, ...), custom_call_target="tpu_custom_call" | custom-call | flops 6000000000 | bytes 32000000 | tf_op jit(solution)/shard_map/global_forward/pallas_call | solution.py:385
  21.0 0.0 copy-done
  21.0 0.6 fusion.2
  22.9 0.6 stack.23.scal
  23.5 0.0 collective-permute-done.4.gains_b.gains_other
  23.5 0.0 copy-start.2
  23.5 0.0 collective-permute-done.1.wo_b.wo_other
  23.5 0.0 collective-permute-done.wq_b.wq_other
  23.5 0.0 copy-start.1
  23.5 0.0 collective-permute-done.2.wu_b.wu_other
  23.5 0.0 collective-permute-done.3.wd_b.wd_other
  23.5 0.5 copy-done.2
  24.1 1.2 copy-done.1
  25.3 38.2 %local_forward.1 = (bf16[1024,768]{1,0:T(8,128)(2,1)}, bf16[1024,768]{1,0:T(8,128)(2,1)}, bf16[1024,768]{1,0:T(8,128)(2,1)}, bf16[1024,2304]{1,0:T(8,128)(2,1)},...) custom-call(s32[5]{0:T(128)} %stack.23.scal, ...), custom_call_target="tpu_custom_call" | custom-call | flops 14499999744 | bytes 60000000 | tf_op jit(solution)/shard_map/local_forward/pallas_call | solution.py:529
  63.5 94.3 %first_part.1 = (f32[48,3072]{1,0:T(8,128)}, f32[192,768]{1,0:T(8,128)}, bf16[1024,768]{1,0:T(8,128)(2,1)}, bf16[1024,2304]{1,0:T(8,128)(2,1)}, f32[1024,768]{1,...) custom-call(bf16[1024,3072]{1,0:T(8,128)(2,1)} %get-tuple-element.56, ...), custom_call_target="tpu_custom_call" | custom-call | flops 35000000512 | bytes 80000000 | tf_op jit(solution)/shard_map/first_part/pallas_call | solution.py:1177
  157.8 102.8 %second_part.1 = (f32[48,2304]{1,0:T(8,128)}, f32[48,768]{1,0:T(8,128)}, f32[48,3072]{1,0:T(8,128)}, f32[192,768]{1,0:T(8,128)}, f32[192,768]{1,0:T(8,128)}, /*i...) custom-call(bf16[4,4,256,192]{3,2,1,0:T(8,128)(2,1)} %get-tuple-element.54.pat, ...), custom_call_target="tpu_custom_call" | custom-call | flops 15000000512 | bytes 60000000 | tf_op jit(solution)/shard_map/second_part/pallas_call | solution.py:1512
  260.7 0.8 fusion.1
  261.5 0.6 fusion
  262.1 7.3 %finish.1 = (f32[2048,768]{1,0:T(8,128)}, bf16[2048,768]{1,0:T(8,128)(2,1)}, f32[192,768]{1,0:T(8,128)}, f32[48,2304]{1,0:T(8,128)}, f32[48,768]{1,0:T(8,128)}, /*index=5*/f32[48,3072]{1,0:T(8,128)}, f32[192,768]{1,0:T(8,128)}) custom-call(bf16[1024,768]{1,0:T(8,128)(2,1)} %get-tuple-element.84.refs_0_, bf16[1024,768]{1,0:T(8,128)(2,1)} %get-tuple-element.85.refs_1_, ...), custom_call_target="tpu_custom_call" | custom-call | flops 1000000 | bytes 20000000 | tf_op jit(solution)/shard_map/finish/pallas_call | solution.py:1567
Async XLA Ops:
  0.6 20.4 %copy-start = (s32[2]{0:T(128)S(1)}, s32[2]{0:T(128)}, u32[]{:S(2)}) copy-start(s32[2]{0:T(128)} %param.10) | copy-start | bytes 28
  0.6 22.9 %collective-permute-start.2 = (bf16[1,768,3072]{2,1,0:T(8,128)(2,1)}, bf16[1,768,3072]{2,1,0:T(8,128)(2,1)}, u32[]{:S(2)}, u32[]{:S(2)}) collective-permute-start(bf16[1,768,3072]{2,1,0:T(8,128)(2,1)} %wu_own.1), channel_id=1, source_target_pairs={{0,16},{16,0},{1,17},{17,1},{2,18},{18,2},{3,19},{19,3},{4,20},{20... | collective-permute-start | bytes 14155784 | tf_op jit(solution)/shard_map/ppermute | solution.py:1584
  0.7 22.8 %collective-permute-start.3 = (bf16[1,3072,768]{2,1,0:T(8,128)(2,1)}, bf16[1,3072,768]{2,1,0:T(8,128)(2,1)}, u32[]{:S(2)}, u32[]{:S(2)}) collective-permute-start(bf16[1,3072,768]{2,1,0:T(8,128)(2,1)} %wd_own.1), channel_id=1, source_target_pairs={{0,16},{16,0},{1,17},{17,1},{2,18},{18,2},{3,19},{19,3},{4,20},{20... | collective-permute-start | bytes 14155784 | tf_op jit(solution)/shard_map/ppermute | solution.py:1584
  1.2 22.3 %collective-permute-start = (bf16[1,768,2304]{2,1,0:T(8,128)(2,1)}, bf16[1,768,2304]{2,1,0:T(8,128)(2,1)S(1)}, u32[]{:S(2)}, u32[]{:S(2)}) collective-permute-start(bf16[1,768,2304]{2,1,0:T(8,128)(2,1)} %wq_own.1), channel_id=1, source_target_pairs={{0,16},{16,0},{1,17},{17,1},{2,18},{18,2},{3,19},{19,3},{4,20},{20... | collective-permute-start | bytes 10616840 | tf_op jit(solution)/shard_map/ppermute | solution.py:1584
  1.3 22.2 %collective-permute-start.1 = (bf16[1,768,768]{2,1,0:T(8,128)(2,1)}, bf16[1,768,768]{2,1,0:T(8,128)(2,1)}, u32[]{:S(2)}, u32[]{:S(2)}) collective-permute-start(bf16[1,768,768]{2,1,0:T(8,128)(2,1)} %wo_own.1), channel_id=1, source_target_pairs={{0,16},{16,0},{1,17},{17,1},{2,18},{18,2},{3,19},{19,3},{4,20},{20... | collective-permute-start | bytes 3538952 | tf_op jit(solution)/shard_map/ppermute | solution.py:1584
  1.7 21.7 %collective-permute-start.4 = (f32[1,2,768]{2,1,0:T(2,128)}, f32[1,2,768]{2,1,0:T(2,128)S(1)}, u32[]{:S(2)}, u32[]{:S(2)}) collective-permute-start(f32[1,2,768]{2,1,0:T(2,128)} %gains_own.1), channel_id=1, source_target_pairs={{0,16},{16,0},{1,17},{17,1},{2,18},{18,2},{3,19},{19,3},{4,20},{20... | collective-permute-start | bytes 18440 | tf_op jit(solution)/shard_map/ppermute | solution.py:1584
  23.5 0.6 copy-start.2
  23.5 1.8 copy-start.1
where the time goes:
time: 271 us; the launch traced here: 270 us
  Pallas kernels  262 us (97%)
  local copies, waits for them, and re-layouts  3.77 us (1%)
    pallas_call x1, Pallas kernels, second_part(): pl.pallas_call(functools.partial(second_kernel, plan=plan), name='second_...  103 us
    pallas_call x1, Pallas kernels, first_part(): pl.pallas_call(functools.partial(first_kernel, plan=plan), name='first_pa...  94.3 us
    pallas_call x1, Pallas kernels, local_forward(): pl.pallas_call(local_forward_kernel, name='local_forward', out_shape=[sds...  38.2 us
    pallas_call x1, Pallas kernels, global_forward(): pl.pallas_call(global_forward_kernel, name='global_forward', out_shape=[s...  19.2 us
    pallas_call x1, Pallas kernels, finish(): pl.pallas_call(finish_kernel, name='finish', out_shape=[sds(*o) for o in...  7.27 us
  transfers between devices with their start and end apart: 5, of which 0 were waited for; matrix products, arithmetic and copies ran while one was open for 0% of the time, Pallas kernels for 7%

commit v1 on v0

--- a/solution.py
+++ b/solution.py
@@ -534,7 +534,7 @@
             num_scalar_prefetch=1,
             grid=(TILES,),
             in_specs=[seq_block(), seq_block(), row_block(TILE // PATCH, D), const_block(1, 2, D)]
-            + [ANY] * 8 + [const_block(1, 2, D)],
+            + [pl.BlockSpec(memory_space=pltpu.HBM)] * 8 + [const_block(1, 2, D)],
             out_specs=[row_block(o[0][0] // TILES, *o[0][1:]) for o in outs],
             scratch_shapes=[
                 WSCRATCH["q"], WSCRATCH["o"], WSCRATCH["u"], WSCRATCH["d"], pltpu.SemaphoreType.DMA((4,)),
@@ -1209,7 +1209,7 @@
     s.xt, s.xo, s.total = alloc((D, SEQ), BF16), alloc((D, SEQ), BF16), alloc((D, UNIT), F32)
     s.pat, s.dpp = alloc((PATCH // 2, 4 * ROWS_G, 192), BF16), alloc((4 * ROWS_G, D), BF16)
     s.xg, s.dy = alloc((2 * ROWS_G, XG), BF16), alloc((2 * ROWS_G, WIDTH_G), BF16)
-    s.gains = alloc((6, 8, D), F32)
+    s.gains = alloc((11, 8, D), F32)
     s.g, s.spread = alloc((ROWS_G, D), BF16), alloc((2, TILE, D), BF16)
     s.wp, s.acc = alloc((2, D, D), BF16), alloc((LANES, SEQ, 128), F32)
     s.specs = alloc.specs
@@ -1235,7 +1235,7 @@
         job_copies(net, b, job, False)
         job.swap_copy = net.remote(b[job.swap].at[0], b[job.swap].at[1], ZN)
     gain_copies = [
-        net.remote(b[s.gains].at[0], b[s.gains].at[i + 1], to) for i, to in enumerate((CORE, X, Y, ZN, ZF))
+        net.remote(b[s.gains].at[i], b[s.gains].at[i + 6], to) for i, to in enumerate((CORE, X, Y, ZN, ZF))
     ]
     dpp_slots = [b[s.dpp].at[i * ROWS_G : i * ROWS_G + ROWS_G, :] for i in range(4)]
     dpp_gives = [net.remote(dpp_in, dpp_slots[0], CORE)] + [net.remote(slot, slot, CORE) for slot in dpp_slots[1:]]
@@ -1278,10 +1278,9 @@
             gain_load.wait()
         else:
             gain_copies[i - 1].wait_recv()
-            b[s.gains][0] = b[s.gains][0] + b[s.gains][i]
+            b[s.gains][i] = b[s.gains][i - 1] + b[s.gains][i + 5]
         if i < 5:
             gain_copies[i].start()
-            gain_copies[i].wait_send()
 
     def forward_dpp():
         def work():
@@ -1406,6 +1405,7 @@
             spread_copy(i).wait()
 
     wp_copy(0).start()
+    gain_step(0)
     g_down, g_up0, g_up1, g_q0, g_q1, g_out = s.glob
     patch = s.patch
     for copy in rest:
@@ -1414,41 +1414,38 @@
     local_products(net, b, [q0], False, xt, total, b[s.a], b[s.dqkv])
     local_products(net, b, [q1], False, xt, total, None, b[s.dqkv])
     local_products(net, b, [proj], False, xo, total, b[s.o], b[s.dr])
-    gain_step(0)
     net.on(0, dpp_load.wait)
     net.on(1, dpp_gives[0].wait_recv)
-    input_grads()
     gain_step(1)
     forward_dpp()
     local_products(net, b, [q0], True, xt, total, None, b[s.dqkv])
     local_products(net, b, [q1], True, xt, total, None, b[s.dqkv])
     local_products(net, b, [proj], True, xo, total, None, b[s.dr])
     net.on(0, first_wait)
-    gain_step(2)
     global_products(g_down)
     patch_products(patch)
     global_products(g_up0)
     advance(b, proj, 0)
     global_products(g_up1)
     advance(b, q0, 0)
+    gain_step(2)
     global_products(g_q0)
     global_products(g_q1)
     global_products(g_out)
+    input_grads()
     net.on(0, spread_rows)
-    gain_step(3)
     advance(b, q1, 0)
     global_advance(g_down, 0)
+    gain_step(3)
     advance(b, patch, 0)
     global_advance(g_up0, 0)
-    gain_step(4)
     global_advance(g_up1, 0)
     advance(b, proj, 1)
     advance(b, proj, 2)
+    gain_step(4)
     advance(b, q0, 1)
     global_advance(g_down, 1)
-    gain_step(5)
     out_patch[...] = last_sum(b, patch)
-    out_gains[...] = b[s.gains][0]
 
     def copy_first():
         out_up[...] = up_in[...]
@@ -1473,6 +1470,8 @@
     global_advance(g_up0, 1)
     stage_four(net, b, q0, out_qkv)
     global_sum(g_q0)
+    gain_step(5)
+    out_gains[...] = b[s.gains][5]
     global_end(g_up1)
     global_sum(g_q1)
     advance(b, q1, 2)
@@ -1493,6 +1492,9 @@
         y_copy.wait_recv()
 
     net.on(1, end_rows)
+
+    for copy in gain_copies:
+        copy.wait_send()
 
     def drain():
         for copy in dpp_gives + dpp_copies + [dyn_copy, y_copy]:

time: 271 us -> 266 us (0.982)
  Pallas kernels: 262 us -> 256 us
    pallas_call x1, Pallas kernels: 103 us -> 97.3 us  [second_part(): pl.pallas_call(functools.partial(second_kernel, plan=plan), name='second_...]
where the time goes in v1:
time: 266 us; the launch traced here: 264 us
  Pallas kernels  256 us (96%)
  local copies, waits for them, and re-layouts  3.77 us (1%)
    pallas_call x1, Pallas kernels, second_part(): pl.pallas_call(functools.partial(second_kernel, plan=plan), name='second_...  97.3 us
    pallas_call x1, Pallas kernels, first_part(): pl.pallas_call(functools.partial(first_kernel, plan=plan), name='first_pa...  94.3 us
    pallas_call x1, Pallas kernels, local_forward(): pl.pallas_call(local_forward_kernel, name='local_forward', out_shape=[sds...  38.2 us
    pallas_call x1, Pallas kernels, global_forward(): pl.pallas_call(global_forward_kernel, name='global_forward', out_shape=[s...  19.2 us
    pallas_call x1, Pallas kernels, finish(): pl.pallas_call(finish_kernel, name='finish', out_shape=[sds(*o) for o in...  7.27 us
  transfers between devices with their start and end apart: 5, of which 0 were waited for; matrix products, arithmetic and copies ran while one was open for 0% of the time, Pallas kernels for 7%

profile of v1, /device:TPU:8, one launch (start us, length us, event | category | flops | bytes accessed | tf_op | source)
XLA Modules:
  0.0 264.1 jit_solution(52753819842779119)
XLA Ops:
  0.6 0.0 copy-start
  0.6 0.1 collective-permute-start.2
  0.7 0.5 collective-permute-start.3
  1.2 0.1 collective-permute-start
  1.3 0.4 collective-permute-start.1
  1.7 0.1 collective-permute-start.4
  1.8 19.2 %global_forward.1 = (bf16[128,768]{1,0:T(8,128)(2,1)}, bf16[256,768]{1,0:T(8,128)(2,1)}, bf16[256,5376]{1,0:T(8,128)(2,1)}, f32[256,768]{1,0:T(8,128)}, bf16[256...) custom-call(bf16[2048,768]{1,0:T(8,128)(2,1)} %states.1, ...), custom_call_target="tpu_custom_call" | custom-call | flops 6000000000 | bytes 32000000 | tf_op jit(solution)/shard_map/global_forward/pallas_call | solution.py:385
  21.0 0.0 copy-done
  21.0 0.6 fusion.2
  22.9 0.6 stack.23.scal
  23.5 0.0 collective-permute-done.4.gains_b.gains_other
  23.5 0.0 copy-start.2
  23.5 0.0 collective-permute-done.1.wo_b.wo_other
  23.5 0.0 collective-permute-done.wq_b.wq_other
  23.5 0.0 copy-start.1
  23.5 0.0 collective-permute-done.2.wu_b.wu_other
  23.5 0.0 collective-permute-done.3.wd_b.wd_other
  23.5 0.5 copy-done.2
  24.1 1.2 copy-done.1
  25.3 38.2 %local_forward.1 = (bf16[1024,768]{1,0:T(8,128)(2,1)}, bf16[1024,768]{1,0:T(8,128)(2,1)}, bf16[1024,768]{1,0:T(8,128)(2,1)}, bf16[1024,2304]{1,0:T(8,128)(2,1)},...) custom-call(s32[5]{0:T(128)} %stack.23.scal, ...), custom_call_target="tpu_custom_call" | custom-call | flops 14499999744 | bytes 60000000 | tf_op jit(solution)/shard_map/local_forward/pallas_call | solution.py:529
  63.5 94.3 %first_part.1 = (f32[48,3072]{1,0:T(8,128)}, f32[192,768]{1,0:T(8,128)}, bf16[1024,768]{1,0:T(8,128)(2,1)}, bf16[1024,2304]{1,0:T(8,128)(2,1)}, f32[1024,768]{1,...) custom-call(bf16[1024,3072]{1,0:T(8,128)(2,1)} %get-tuple-element.56, ...), custom_call_target="tpu_custom_call" | custom-call | flops 35000000512 | bytes 80000000 | tf_op jit(solution)/shard_map/first_part/pallas_call | solution.py:1177
  157.8 97.3 %second_part.1 = (f32[48,2304]{1,0:T(8,128)}, f32[48,768]{1,0:T(8,128)}, f32[48,3072]{1,0:T(8,128)}, f32[192,768]{1,0:T(8,128)}, f32[192,768]{1,0:T(8,128)}, /*i...) custom-call(bf16[4,4,256,192]{3,2,1,0:T(8,128)(2,1)} %get-tuple-element.54.pat, ...), custom_call_target="tpu_custom_call" | custom-call | flops 15000000512 | bytes 60000000 | tf_op jit(solution)/shard_map/second_part/pallas_call | solution.py:1514
  255.2 0.8 fusion.1
  256.0 0.6 fusion
  256.6 7.3 %finish.1 = (f32[2048,768]{1,0:T(8,128)}, bf16[2048,768]{1,0:T(8,128)(2,1)}, f32[192,768]{1,0:T(8,128)}, f32[48,2304]{1,0:T(8,128)}, f32[48,768]{1,0:T(8,128)}, /*index=5*/f32[48,3072]{1,0:T(8,128)}, f32[192,768]{1,0:T(8,128)}) custom-call(bf16[1024,768]{1,0:T(8,128)(2,1)} %get-tuple-element.84.refs_0_, bf16[1024,768]{1,0:T(8,128)(2,1)} %get-tuple-element.85.refs_1_, ...), custom_call_target="tpu_custom_call" | custom-call | flops 1000000 | bytes 20000000 | tf_op jit(solution)/shard_map/finish/pallas_call | solution.py:1569
Async XLA Ops:
  0.6 20.4 %copy-start = (s32[2]{0:T(128)S(1)}, s32[2]{0:T(128)}, u32[]{:S(2)}) copy-start(s32[2]{0:T(128)} %param.10) | copy-start | bytes 28
  0.6 22.9 %collective-permute-start.2 = (bf16[1,768,3072]{2,1,0:T(8,128)(2,1)}, bf16[1,768,3072]{2,1,0:T(8,128)(2,1)}, u32[]{:S(2)}, u32[]{:S(2)}) collective-permute-start(bf16[1,768,3072]{2,1,0:T(8,128)(2,1)} %wu_own.1), channel_id=1, source_target_pairs={{0,16},{16,0},{1,17},{17,1},{2,18},{18,2},{3,19},{19,3},{4,20},{20... | collective-permute-start | bytes 14155784 | tf_op jit(solution)/shard_map/ppermute | solution.py:1586
  0.7 22.8 %collective-permute-start.3 = (bf16[1,3072,768]{2,1,0:T(8,128)(2,1)}, bf16[1,3072,768]{2,1,0:T(8,128)(2,1)}, u32[]{:S(2)}, u32[]{:S(2)}) collective-permute-start(bf16[1,3072,768]{2,1,0:T(8,128)(2,1)} %wd_own.1), channel_id=1, source_target_pairs={{0,16},{16,0},{1,17},{17,1},{2,18},{18,2},{3,19},{19,3},{4,20},{20... | collective-permute-start | bytes 14155784 | tf_op jit(solution)/shard_map/ppermute | solution.py:1586
  1.2 22.3 %collective-permute-start = (bf16[1,768,2304]{2,1,0:T(8,128)(2,1)}, bf16[1,768,2304]{2,1,0:T(8,128)(2,1)S(1)}, u32[]{:S(2)}, u32[]{:S(2)}) collective-permute-start(bf16[1,768,2304]{2,1,0:T(8,128)(2,1)} %wq_own.1), channel_id=1, source_target_pairs={{0,16},{16,0},{1,17},{17,1},{2,18},{18,2},{3,19},{19,3},{4,20},{20... | collective-permute-start | bytes 10616840 | tf_op jit(solution)/shard_map/ppermute | solution.py:1586
  1.3 22.2 %collective-permute-start.1 = (bf16[1,768,768]{2,1,0:T(8,128)(2,1)}, bf16[1,768,768]{2,1,0:T(8,128)(2,1)}, u32[]{:S(2)}, u32[]{:S(2)}) collective-permute-start(bf16[1,768,768]{2,1,0:T(8,128)(2,1)} %wo_own.1), channel_id=1, source_target_pairs={{0,16},{16,0},{1,17},{17,1},{2,18},{18,2},{3,19},{19,3},{4,20},{20... | collective-permute-start | bytes 3538952 | tf_op jit(solution)/shard_map/ppermute | solution.py:1586
  1.7 21.7 %collective-permute-start.4 = (f32[1,2,768]{2,1,0:T(2,128)}, f32[1,2,768]{2,1,0:T(2,128)S(1)}, u32[]{:S(2)}, u32[]{:S(2)}) collective-permute-start(f32[1,2,768]{2,1,0:T(2,128)} %gains_own.1), channel_id=1, source_target_pairs={{0,16},{16,0},{1,17},{17,1},{2,18},{18,2},{3,19},{19,3},{4,20},{20... | collective-permute-start | bytes 18440 | tf_op jit(solution)/shard_map/ppermute | solution.py:1586
  23.5 0.6 copy-start.2
  23.5 1.8 copy-start.1
